TPU v7x, 512 devices: a whole 4x4x16 slice. The times are simulated.
512 devices in a mesh: sec: 64 (over y, z), mpo: 8 (over x, core).
Axes of the slice: x: 4, y: 4, z: 16, core: 2. Of those that a mesh axis runs over, the one named last changes fastest.
Arguments:
- wavefunction: bfloat16 [64, 8, 512, 256], P('sec', None, 'mpo'), may hold values from -6 to 6
- left_env: bfloat16 [64, 40, 512, 512], P('sec', 'mpo'), may hold values from -0.0390625 to 0.0390625
- right_env: bfloat16 [64, 40, 256, 256], P('sec', 'mpo'), may hold values from -0.375 to 0.375
- left_dims: int32 [64], P('sec'), may hold values from 256 to 512
- right_dims: int32 [64], P('sec'), may hold values from 128 to 256
- term_shift: int32 [40], P('mpo'), may hold values from 0 to 4, as said below
Outputs:
- product: bfloat16 [64, 8, 512, 256], P('sec', None, 'mpo')
Inputs may be any that keep to these rules, and one draw needn't show every extreme that they name: `term_shift`: each of the five classes is named by exactly 8 terms.
All inputs are finite; a program needn't handle non-finite values.
Results may differ from a plain program's by a relative error of at most 0.0049.
Values may be sent and summed in bfloat16 or wider, within the bound.
A program may use at most 64 MiB of HBM per device.

v0:
```python
import jax
import jax.numpy as jnp
from jax import lax
from jax.sharding import PartitionSpec as P

SPINS = 8
number_steps = (0, 1, -1, 1, -1)
spin_steps = (0, 1, -1, -1, 1)


def shifted(array, axis, by):
    length = lax.axis_size(axis)
    pairs = [(i, i + by) for i in range(length) if 0 <= i + by < length]
    return lax.ppermute(array, axis, pairs)


def per_device(wavefunction, left_env, right_env, left_dims, right_dims, term_shift):
    row_share = wavefunction.shape[2]
    columns = wavefunction.shape[3]
    mpo_place = lax.axis_index("mpo")
    sector_id = lax.axis_index("sec")
    lattice_rows = lax.axis_size("sec") // SPINS
    rows_here = mpo_place * row_share + jnp.arange(row_share, dtype=jnp.int32)
    column_ids = jnp.arange(columns, dtype=jnp.int32)
    keep_mask = (rows_here[:, None] < left_dims[0]) & (column_ids[None, :] < right_dims[0])
    live_block = jnp.where(keep_mask[None, None], wavefunction, jnp.zeros_like(wavefunction))
    sector_line = sector_id // SPINS
    sector_place = sector_id % SPINS
    line_steps = jnp.array(number_steps, dtype=jnp.int32)
    place_steps = jnp.array(spin_steps, dtype=jnp.int32)
    source_line = sector_line - line_steps
    source_place = sector_place - place_steps
    inside = (
        (source_line >= 0)
        & (source_line < lattice_rows)
        & (source_place >= 0)
        & (source_place < SPINS)
    )
    selector = (
        (term_shift[:, None] == jnp.arange(5, dtype=jnp.int32)[None, :]) & inside[None, :]
    ).astype(jnp.bfloat16)
    full_block = lax.all_gather(live_block, "mpo", axis=2, tiled=True)
    neighbours = [full_block]
    for shift_class in range(1, 5):
        offset = number_steps[shift_class] * SPINS + spin_steps[shift_class]
        neighbours.append(shifted(full_block, "sec", offset))
    stacked = jnp.concatenate(neighbours, axis=0)
    selected = jnp.einsum(
        "tc,cvpq->tvpq", selector, stacked, preferred_element_type=jnp.float32
    ).astype(jnp.bfloat16)
    left_terms = left_env[0]
    right_terms = right_env[0]
    applied = jnp.einsum(
        "tpk,tvkq->tvpq", left_terms, selected, preferred_element_type=jnp.float32
    ).astype(jnp.bfloat16)
    term_total = jnp.einsum(
        "tvpk,tqk->vpq", applied, right_terms, preferred_element_type=jnp.float32
    )[None]
    row_sums = lax.psum_scatter(term_total, "mpo", scatter_dimension=2, tiled=True)
    return jnp.where(keep_mask[None, None], row_sums, jnp.zeros_like(row_sums)).astype(jnp.bfloat16)


def solution(mesh):
    in_specs = (
        P("sec", None, "mpo", None),
        P("sec", "mpo", None, None),
        P("sec", "mpo", None, None),
        P("sec"),
        P("sec"),
        P("mpo"),
    )
    out_specs = P("sec", None, "mpo", None)
    return jax.shard_map(
        per_device, mesh=mesh, in_specs=in_specs, out_specs=out_specs, check_vma=False
    )
```

profile of v0, /device:TPU:8, one launch (start us, length us, event | category | flops | bytes accessed | tf_op | source)
XLA Modules:
  0.0 792.9 jit_solution(16231609190747013689)
XLA Ops:
  8.0 0.1 broadcast_and_fusion
  8.1 1.7 broadcast_select_fusion
  9.8 0.0 all-gather.2.cloned.1.call-update
  9.8 0.0 reduce-scatter.2.cloned.1.call-start
  9.9 37.4 %all-gather.2.cloned.1.call-done = bf16[1,8,512,256]{3,2,1,0:T(8,128)(2,1)} async-done(((bf16[1,8,64,256]{3,2,1,0:T(8,128)(2,1)}), bf16[1,8,512,256]{3,2,1,0:T(8,128)(2,1)}) %all-gather.2.cloned.1.call-update) | async-done | bytes 2097168 | tf_op jit(solution)/shard_map/all_gather | solution.py:42
  47.3 12.0 %collective-permute-start = (bf16[1,8,512,256]{3,2,1,0:T(8,128)(2,1)}, bf16[1,8,512,256]{3,2,1,0:T(8,128)(2,1)}, u32[]{:S(2)}, u32[]{:S(2)}) collective-permute-start(bf16[1,8,512,256]{3,2,1,0:T(8,128)(2,1)} %all-gather.2.cloned.1.call-done), channel_id=1, source_target_pairs={{0,72},{8,80},{16,88},{24,96},{32,104},{40,112},{48,120},{56,128},... | collective-permute-start | bytes 6291464 | tf_op jit(solution)/shard_map/ppermute | solution.py:14
  59.3 2.7 collective-permute-start.1
  62.0 10.5 %collective-permute-start.2 = (bf16[1,8,512,256]{3,2,1,0:T(8,128)(2,1)}, bf16[1,8,512,256]{3,2,1,0:T(8,128)(2,1)}, u32[]{:S(2)}, u32[]{:S(2)}) collective-permute-start(bf16[1,8,512,256]{3,2,1,0:T(8,128)(2,1)} %all-gather.2.cloned.1.call-done), channel_id=1, source_target_pairs={{0,56},{8,64},{16,72},{24,80},{32,88},{40,96},{48,104},{56,112},{6... | collective-permute-start | bytes 6291464 | tf_op jit(solution)/shard_map/ppermute | solution.py:14
  72.5 4.0 collective-permute-start.3
  76.6 0.7 compare_and_fusion
  77.2 1.7 constant_dynamic-update-slice_fusion.4
  79.0 311.9 %collective-permute-done = bf16[1,8,512,256]{3,2,1,0:T(8,128)(2,1)} collective-permute-done((bf16[1,8,512,256]{3,2,1,0:T(8,128)(2,1)}, bf16[1,8,512,256]{3,2,1,0:T(8,128)(2,1)}, u32[]{:S(2)}, u32[]{:S(2)}) %collective-permute-start) | collective-permute-done | bytes 2097184 | tf_op jit(solution)/shard_map/ppermute | solution.py:14
  390.9 1.7 constant_dynamic-update-slice_fusion.3
  392.6 0.0 collective-permute-done.1
  392.7 1.7 constant_dynamic-update-slice_fusion.2
  394.4 296.8 %collective-permute-done.2 = bf16[1,8,512,256]{3,2,1,0:T(8,128)(2,1)} collective-permute-done((bf16[1,8,512,256]{3,2,1,0:T(8,128)(2,1)}, bf16[1,8,512,256]{3,2,1,0:T(8,128)(2,1)}, u32[]{:S(2)}, u32[]{:S(2)}) %collective-permute-start.2) | collective-permute-done | bytes 2097184 | tf_op jit(solution)/shard_map/ppermute | solution.py:14
  691.2 1.7 constant_dynamic-update-slice_fusion.1
  692.9 1.7 constant_dynamic-update-slice_fusion
  694.7 0.0 copy-start.2
  694.7 24.2 %fusion = bf16[5,8,512,256]{3,0,2,1:T(8,128)(2,1)} fusion(bf16[5,8,512,256]{3,2,1,0:T(8,128)(2,1)S(1)} %constant_dynamic-update-slice_fusion, s32[5]{0:T(128)S(1)} %copy-done.1, pred[5]{0:T(512)(128)(4,1)S(1)} %compare_and_fusion), kind=kOutput, calls=%fused_computation.1 | convolution fusion | flops 52428848 | bytes 20971544 | tf_op jit(solution)/shard_map/tc,cvpq->tvpq/dot_general | solution.py:48
  718.9 16.6 %fusion.13 = f32[1,8,512,256]{3,2,1,0:T(8,128)} fusion(bf16[1,5,512,512]{3,2,1,0:T(8,128)(2,1)S(1)} %copy-done, bf16[1,5,256,256]{3,2,1,0:T(8,128)(2,1)S(1)} %copy-done.2, bf16[5,8,512,256]{3,0,2,1:T(8,128)(2,1)} %fusion), kind=kOutput, calls=%fused_computation.9 | convolution fusion | flops 8058306560 | bytes 17956864 | tf_op jit(solution)/shard_map/tvpk,tqk->vpq/dot_general | solution.py:56
  735.5 0.0 reduce-scatter.2.cloned.1.call-update
  735.5 48.7 %reduce-scatter.2.cloned.1.call-done = f32[1,8,64,256]{3,2,1,0:T(8,128)} async-done(((f32[1,8,512,256]{3,2,1,0:T(8,128)}), f32[1,8,64,256]{3,2,1,0:T(8,128)}) %reduce-scatter.2.cloned.1.call-update) | async-done | bytes 524304 | tf_op jit(solution)/shard_map/reduce_scatter | solution.py:59
  784.3 1.8 select_convert_fusion
  (9 shorter events, 0.0 us)
Async XLA Ops:
  6.5 712.4 %copy-start = (bf16[1,5,512,512]{3,2,1,0:T(8,128)(2,1)S(1)}, bf16[1,5,512,512]{3,2,1,0:T(8,128)(2,1)}, u32[]{:S(2)}) copy-start(bf16[1,5,512,512]{3,2,1,0:T(8,128)(2,1)} %param.9) | copy-start | bytes 7864324
  6.5 40.8 %all-gather.2.cloned.1.call-start = ((), (), s32[]{:S(2)}) async-start(), calls=%async_computation.1 | async-start | bytes 2359296 | tf_op jit(solution)/shard_map/all_gather | solution.py:42
  9.8 774.5 %reduce-scatter.2.cloned.1.call-start = ((), (), s32[]{:S(2)}) async-start(), calls=%async_computation.2 | async-start | bytes 4718592 | tf_op jit(solution)/shard_map/reduce_scatter | solution.py:59
  47.3 343.6 %collective-permute-start = (bf16[1,8,512,256]{3,2,1,0:T(8,128)(2,1)}, bf16[1,8,512,256]{3,2,1,0:T(8,128)(2,1)}, u32[]{:S(2)}, u32[]{:S(2)}) collective-permute-start(bf16[1,8,512,256]{3,2,1,0:T(8,128)(2,1)} %all-gather.2.cloned.1.call-done), channel_id=1, source_target_pairs={{0,72},{8,80},{16,88},{24,96},{32,104},{40,112},{48,120},{56,128},... | collective-permute-start | bytes 6291464 | tf_op jit(solution)/shard_map/ppermute | solution.py:14
  59.3 333.4 %collective-permute-start.1 = (bf16[1,8,512,256]{3,2,1,0:T(8,128)(2,1)}, bf16[1,8,512,256]{3,2,1,0:T(8,128)(2,1)}, u32[]{:S(2)}, u32[]{:S(2)}) collective-permute-start(bf16[1,8,512,256]{3,2,1,0:T(8,128)(2,1)} %all-gather.2.cloned.1.call-done), channel_id=1, source_target_pairs={{72,0},{80,8},{88,16},{96,24},{104,32},{112,40},{120,48},{128,56},... | collective-permute-start | bytes 6291464 | tf_op jit(solution)/shard_map/ppermute | solution.py:14
  62.0 629.2 %collective-permute-start.2 = (bf16[1,8,512,256]{3,2,1,0:T(8,128)(2,1)}, bf16[1,8,512,256]{3,2,1,0:T(8,128)(2,1)}, u32[]{:S(2)}, u32[]{:S(2)}) collective-permute-start(bf16[1,8,512,256]{3,2,1,0:T(8,128)(2,1)} %all-gather.2.cloned.1.call-done), channel_id=1, source_target_pairs={{0,56},{8,64},{16,72},{24,80},{32,88},{40,96},{48,104},{56,112},{6... | collective-permute-start | bytes 6291464 | tf_op jit(solution)/shard_map/ppermute | solution.py:14
  72.5 620.5 %collective-permute-start.3 = (bf16[1,8,512,256]{3,2,1,0:T(8,128)(2,1)}, bf16[1,8,512,256]{3,2,1,0:T(8,128)(2,1)}, u32[]{:S(2)}, u32[]{:S(2)}) collective-permute-start(bf16[1,8,512,256]{3,2,1,0:T(8,128)(2,1)} %all-gather.2.cloned.1.call-done), channel_id=1, source_target_pairs={{56,0},{64,8},{72,16},{80,24},{88,32},{96,40},{104,48},{112,56},{1... | collective-permute-start | bytes 6291464 | tf_op jit(solution)/shard_map/ppermute | solution.py:14
  77.2 617.4 %copy-start.1 = (s32[5]{0:T(128)S(1)}, s32[5]{0:T(128)}, u32[]{:S(2)}) copy-start(s32[5]{0:T(128)} %param.13) | copy-start | bytes 64
  694.7 24.2 %copy-start.2 = (bf16[1,5,256,256]{3,2,1,0:T(8,128)(2,1)S(1)}, bf16[1,5,256,256]{3,2,1,0:T(8,128)(2,1)}, u32[]{:S(2)}) copy-start(bf16[1,5,256,256]{3,2,1,0:T(8,128)(2,1)} %param.10) | copy-start | bytes 1966084
Sparse Core Ops, SparseCore 0:
  9.9 37.3 all-gather.1
  735.7 48.5 reduce-scatter.1
where the time goes:
time: 793 us
  waiting for transfers between devices  695 us (88%)
  matrix products  40.8 us (5%)
  starting transfers between devices  29.3 us (4%)
  between operations  15 us (2%)
  local copies, waits for them, and re-layouts  8.71 us (1%)
    ppermute x4, waiting for transfers between devices, shifted(): return lax.ppermute(array, axis, pairs)  609 us
    reduce_scatter x1, waiting for transfers between devices, per_device(): lax.psum_scatter(term_total, 'mpo', scatter_dimension=2, tiled=True)  48.7 us
    all_gather x1, waiting for transfers between devices, per_device(): full_block = lax.all_gather(live_block, 'mpo', axis=2, tiled=True)  37.4 us
    ppermute x4, starting transfers between devices, shifted(): return lax.ppermute(array, axis, pairs)  29.2 us
    dot_general x1, matrix products, per_device(): jnp.einsum('tc,cvpq->tvpq', selector, stacked, preferred_element_type=jnp...  24.2 us
    dot_general x1, matrix products, per_device(): jnp.einsum('tvpk,tqk->vpq', applied, right_terms, preferred_element_type=...  16.6 us
  transfers between devices with their start and end apart: 6, of which 4 were waited for; matrix products, arithmetic and copies ran while one was open for 1% of the time, Pallas kernels for 0%

commit v1 on v0

--- a/solution.py
+++ b/solution.py
@@ -39,7 +39,8 @@
     selector = (
         (term_shift[:, None] == jnp.arange(5, dtype=jnp.int32)[None, :]) & inside[None, :]
     ).astype(jnp.bfloat16)
-    full_block = lax.all_gather(live_block, "mpo", axis=2, tiled=True)
+    repeated = jnp.stack([live_block] * lax.axis_size("mpo"))
+    full_block = jnp.concatenate(lax.all_to_all(repeated, "mpo", 0, 0), axis=2)
     neighbours = [full_block]
     for shift_class in range(1, 5):
         offset = number_steps[shift_class] * SPINS + spin_steps[shift_class]

time: 793 us -> 877 us (1.11); the launches traced: 793 us -> 868 us
  local copies, waits for them, and re-layouts: 8.71 us -> 112 us
  waiting for transfers between devices: 695 us -> 642 us
  blocking collectives: 0 us -> 31.3 us
    concatenate x1, local copies, waits for them, and re-layouts: 1.74 us -> 74.4 us  [per_device(): stacked = jnp.concatenate(neighbours, axis=0)]
    all_gather x1 -> x0, waiting for transfers between devices: 37.4 us -> none  [per_device(): full_block = lax.all_gather(live_block, 'mpo', axis=2, tiled=True)]
    all_to_all x0 -> x1, blocking collectives: none -> 31.3 us  [per_device(): full_block = jnp.concatenate(lax.all_to_all(repeated, 'mpo', 0, 0), axis=2)]
    ppermute x0 -> x4, local copies, waits for them, and re-layouts: none -> 28.5 us  [shifted(): return lax.ppermute(array, axis, pairs)]
    dot_general x1, matrix products: 24.2 us -> 14.9 us  [per_device(): jnp.einsum('tc,cvpq->tvpq', selector, stacked, preferred_element_type=jnp...]
  transfers between devices with their start and end apart: 6 -> 5, of which waited for: 4 -> 4; matrix products, arithmetic and copies ran while one was open for 1% -> 3% of each run, Pallas kernels for 0% -> 0%
where the time goes in v1:
time: 877 us; the launch traced here: 868 us
  waiting for transfers between devices  642 us (73%)
  local copies, waits for them, and re-layouts  112 us (13%)
  matrix products  33.1 us (4%)
  starting transfers between devices  31.7 us (4%)
  blocking collectives  31.3 us (4%)
  between operations  15 us (2%)
    ppermute x4, waiting for transfers between devices, shifted(): return lax.ppermute(array, axis, pairs)  601 us
    concatenate x1, local copies, waits for them, and re-layouts, per_device(): stacked = jnp.concatenate(neighbours, axis=0)  74.4 us
    reduce_scatter x1, waiting for transfers between devices, per_device(): lax.psum_scatter(term_total, 'mpo', scatter_dimension=2, tiled=True)  41.2 us
    ppermute x4, starting transfers between devices, shifted(): return lax.ppermute(array, axis, pairs)  31.7 us
    all_to_all x1, blocking collectives, per_device(): full_block = jnp.concatenate(lax.all_to_all(repeated, 'mpo', 0, 0), axis=2)  31.3 us
    ppermute x4, local copies, waits for them, and re-layouts, shifted(): return lax.ppermute(array, axis, pairs)  28.5 us
    dot_general x1, matrix products, per_device(): jnp.einsum('tvpk,tqk->vpq', applied, right_terms, preferred_element_type=...  18.2 us
  transfers between devices with their start and end apart: 5, of which 4 were waited for; matrix products, arithmetic and copies ran while one was open for 3% of the time, Pallas kernels for 0%

profile of v1, /device:TPU:8, one launch (start us, length us, event | category | flops | bytes accessed | tf_op | source)
XLA Modules:
  0.0 867.5 jit_solution(4606943991521428210)
XLA Ops:
  8.0 0.1 broadcast_and_fusion
  8.1 1.0 select_bitcast_fusion
  9.1 0.2 stack.2
  9.3 0.0 copy-start.2
  9.4 31.3 %all_to_all.5 = bf16[8,1,8,64,256]{4,3,2,1,0:T(8,128)(2,1)S(1)} all-to-all(bf16[8,1,8,64,256]{4,3,2,1,0:T(8,128)(2,1)S(1)} %stack.2), channel_id=1, replica_groups=mesh['sec'=64,'mpo'=8] {'mpo'}, dimensions={0} | all-to-all | bytes 4194304 | tf_op jit(solution)/shard_map/all_to_all | solution.py:43
  40.7 1.5 copy.17
  42.1 15.2 %collective-permute-start.3 = (bf16[1,8,512,256]{3,2,1,0:T(8,128)(2,1)}, bf16[1,8,512,256]{3,2,1,0:T(8,128)(2,1)}, u32[]{:S(2)}, u32[]{:S(2)}) collective-permute-start(bf16[1,8,512,256]{3,2,1,0:T(8,128)(2,1)} %bitcast.6), channel_id=1, source_target_pairs={{56,0},{64,8},{72,16},{80,24},{88,32},{96,40},{104,48},{112,56},{1... | collective-permute-start | bytes 6291464 | tf_op jit(solution)/shard_map/ppermute | solution.py:14
  57.3 1.9 collective-permute-start.2
  59.2 9.6 %collective-permute-start.1 = (bf16[1,8,512,256]{3,2,1,0:T(8,128)(2,1)}, bf16[1,8,512,256]{3,2,1,0:T(8,128)(2,1)}, u32[]{:S(2)}, u32[]{:S(2)}) collective-permute-start(bf16[1,8,512,256]{3,2,1,0:T(8,128)(2,1)} %bitcast.6), channel_id=1, source_target_pairs={{72,0},{80,8},{88,16},{96,24},{104,32},{112,40},{120,48},{128,56},... | collective-permute-start | bytes 6291464 | tf_op jit(solution)/shard_map/ppermute | solution.py:14
  68.9 5.1 collective-permute-start
  74.0 7.0 copy.18
  81.0 293.1 %collective-permute-done.3 = bf16[1,8,512,256]{3,2,1,0:T(8,128)(2,1)} collective-permute-done((bf16[1,8,512,256]{3,2,1,0:T(8,128)(2,1)}, bf16[1,8,512,256]{3,2,1,0:T(8,128)(2,1)}, u32[]{:S(2)}, u32[]{:S(2)}) %collective-permute-start.3) | collective-permute-done | bytes 2097184 | tf_op jit(solution)/shard_map/ppermute | solution.py:14
  374.1 7.1 copy.22
  381.2 7.1 collective-permute-done.2
  388.3 7.1 copy.21
  395.3 300.6 %collective-permute-done.1 = bf16[1,8,512,256]{3,2,1,0:T(8,128)(2,1)} collective-permute-done((bf16[1,8,512,256]{3,2,1,0:T(8,128)(2,1)}, bf16[1,8,512,256]{3,2,1,0:T(8,128)(2,1)}, u32[]{:S(2)}, u32[]{:S(2)}) %collective-permute-start.1) | collective-permute-done | bytes 2097184 | tf_op jit(solution)/shard_map/ppermute | solution.py:14
  695.9 7.2 copy.20
  703.1 7.2 copy.19
  710.3 74.4 %concatenate.3 = bf16[5,8,512,256]{3,0,2,1:T(8,128)(2,1)} concatenate(bf16[1,8,512,256]{3,0,2,1:T(2,128)(2,1)} %copy.18, bf16[1,8,512,256]{3,0,2,1:T(2,128)(2,1)} %copy.19, bf16[1,8,512,256]{3,0,2,1:T(2,128)(2,1)} %copy.20, bf16[1,8,512,256]{3,0,2,1:T(2,128)(2,1)} %copy.21, bf16[1,8,512,256]{3,0,2,1:T(2,128)(2,1)} %copy.22), dimensions={0} | concatenate | bytes 20971520 | tf_op jit(solution)/shard_map/concatenate | solution.py:48
  784.7 14.9 %convolution_convert_fusion = bf16[5,8,512,256]{3,0,2,1:T(8,128)(2,1)} fusion(bf16[5,8,512,256]{3,0,2,1:T(8,128)(2,1)} %concatenate.3, s32[5]{0:T(128)S(1)} %copy-done.1, pred[5]{0:T(512)(128)(4,1)S(1)} %compare_and_fusion), kind=kOutput, calls=%fused_computation.5 | convolution fusion | flops 57671728 | bytes 20971544 | tf_op jit(solution)/shard_map/tc,cvpq->tvpq/dot_general | solution.py:49
  799.5 18.2 %fusion.11 = f32[1,8,512,256]{3,2,1,0:T(8,128)} fusion(bf16[5,8,512,256]{3,0,2,1:T(8,128)(2,1)} %convolution_convert_fusion, bf16[1,5,512,512]{3,2,1,0:T(8,128)(2,1)S(1)} %copy-done, bf16[1,5,256,256]{3,2,1,0:T(8,128)(2,1)S(1)} %copy-done.4), kind=kOutput, calls=%fused_computation.7 | convolution fusion | flops 8058306560 | bytes 17956864 | tf_op jit(solution)/shard_map/tvpk,tqk->vpq/dot_general | solution.py:57
  817.7 0.0 reduce-scatter.2.cloned.1.call-update
  817.7 41.2 %reduce-scatter.2.cloned.1.call-done = f32[1,8,64,256]{3,2,1,0:T(8,128)} async-done(((f32[1,8,512,256]{3,2,1,0:T(8,128)}), f32[1,8,64,256]{3,2,1,0:T(8,128)}) %reduce-scatter.2.cloned.1.call-update) | async-done | bytes 524304 | tf_op jit(solution)/shard_map/reduce_scatter | solution.py:60
  858.9 1.8 select_convert_fusion
  (14 shorter events, 0.0 us)
Async XLA Ops:
  6.5 793.0 %copy-start = (bf16[1,5,512,512]{3,2,1,0:T(8,128)(2,1)S(1)}, bf16[1,5,512,512]{3,2,1,0:T(8,128)(2,1)}, u32[]{:S(2)}) copy-start(bf16[1,5,512,512]{3,2,1,0:T(8,128)(2,1)} %param.9) | copy-start | bytes 7864324
  6.5 852.4 %reduce-scatter.2.cloned.1.call-start = ((), (), s32[]{:S(2)}) async-start(), calls=%async_computation.2 | async-start | bytes 4718592 | tf_op jit(solution)/shard_map/reduce_scatter | solution.py:60
  9.3 64.6 %copy-start.2 = (s32[5]{0:T(128)S(1)}, s32[5]{0:T(128)}, u32[]{:S(2)}) copy-start(s32[5]{0:T(128)} %constant.56) | copy-start | bytes 64
  9.3 64.6 %copy-start.3 = (s32[5]{0:T(128)S(1)}, s32[5]{0:T(128)}, u32[]{:S(2)}) copy-start(s32[5]{0:T(128)} %constant.55) | copy-start | bytes 64
  42.1 332.0 %collective-permute-start.3 = (bf16[1,8,512,256]{3,2,1,0:T(8,128)(2,1)}, bf16[1,8,512,256]{3,2,1,0:T(8,128)(2,1)}, u32[]{:S(2)}, u32[]{:S(2)}) collective-permute-start(bf16[1,8,512,256]{3,2,1,0:T(8,128)(2,1)} %bitcast.6), channel_id=1, source_target_pairs={{56,0},{64,8},{72,16},{80,24},{88,32},{96,40},{104,48},{112,56},{1... | collective-permute-start | bytes 6291464 | tf_op jit(solution)/shard_map/ppermute | solution.py:14
  57.3 331.0 %collective-permute-start.2 = (bf16[1,8,512,256]{3,2,1,0:T(8,128)(2,1)}, bf16[1,8,512,256]{3,2,1,0:T(8,128)(2,1)}, u32[]{:S(2)}, u32[]{:S(2)}) collective-permute-start(bf16[1,8,512,256]{3,2,1,0:T(8,128)(2,1)} %bitcast.6), channel_id=1, source_target_pairs={{0,56},{8,64},{16,72},{24,80},{32,88},{40,96},{48,104},{56,112},{6... | collective-permute-start | bytes 6291464 | tf_op jit(solution)/shard_map/ppermute | solution.py:14
  59.2 636.7 %collective-permute-start.1 = (bf16[1,8,512,256]{3,2,1,0:T(8,128)(2,1)}, bf16[1,8,512,256]{3,2,1,0:T(8,128)(2,1)}, u32[]{:S(2)}, u32[]{:S(2)}) collective-permute-start(bf16[1,8,512,256]{3,2,1,0:T(8,128)(2,1)} %bitcast.6), channel_id=1, source_target_pairs={{72,0},{80,8},{88,16},{96,24},{104,32},{112,40},{120,48},{128,56},... | collective-permute-start | bytes 6291464 | tf_op jit(solution)/shard_map/ppermute | solution.py:14
  68.9 634.2 %collective-permute-start = (bf16[1,8,512,256]{3,2,1,0:T(8,128)(2,1)}, bf16[1,8,512,256]{3,2,1,0:T(8,128)(2,1)}, u32[]{:S(2)}, u32[]{:S(2)}) collective-permute-start(bf16[1,8,512,256]{3,2,1,0:T(8,128)(2,1)} %bitcast.6), channel_id=1, source_target_pairs={{0,72},{8,80},{16,88},{24,96},{32,104},{40,112},{48,120},{56,128},... | collective-permute-start | bytes 6291464 | tf_op jit(solution)/shard_map/ppermute | solution.py:14
  710.3 74.4 %copy-start.1 = (s32[5]{0:T(128)S(1)}, s32[5]{0:T(128)}, u32[]{:S(2)}) copy-start(s32[5]{0:T(128)} %param.13) | copy-start | bytes 64
  784.7 14.9 %copy-start.4 = (bf16[1,5,256,256]{3,2,1,0:T(8,128)(2,1)S(1)}, bf16[1,5,256,256]{3,2,1,0:T(8,128)(2,1)}, u32[]{:S(2)}) copy-start(bf16[1,5,256,256]{3,2,1,0:T(8,128)(2,1)} %param.10) | copy-start | bytes 1966084
Sparse Core Ops, SparseCore 0:
  817.9 40.9 reduce-scatter.1
